TPU v7x, 128 devices: a whole 4x4x4 slice. The times are simulated.
128 devices in a mesh: walk: 8 (over x, core), blk: 16 (over y, z).
Axes of the slice: x: 4, y: 4, z: 4, core: 2. Of those that a mesh axis runs over, the one named last changes fastest.
Arguments:
- derivs: bfloat16 [1536, 409600], P('walk', 'blk'), may hold values from -0.5 to 1.5
- energy_grads: bfloat16 [1536, 409600], P('walk', 'blk'), may hold values from -0.5 to 1.5
- local_energy: float32 [1536], P('walk'), may hold values from -6 to 6
- directions: bfloat16 [512, 25600], P('blk'), may hold values from -0.0390625 to 0.0390625
- widths: int32 [16], P('blk'), may hold values from 6400 to 25600, as said below
- live_rows: int32 [8], P('walk'), may hold values from 96 to 192, as said below
Outputs:
- hamiltonian: float32 [512, 512], P('blk', 'walk')
- correlation: float32 [512, 512], P('blk', 'walk')
Inputs may be any that keep to these rules, and one draw needn't show every extreme that they name: `widths`: each block uses between a quarter of its 25600 slots and all of them; some block uses all 25600. `live_rows`: each group has at least half of its 192 slots live; some group has all 192 live.
All inputs are finite; a program needn't handle non-finite values.
Results may differ from a plain program's by a relative error of at most 0.0041.
Values may be sent and summed in bfloat16 or wider, within the bound.
A program may use at most 64 MiB of HBM per device.

v0:
```python
import jax
import jax.numpy as jnp
from jax import lax
from jax.sharding import PartitionSpec as P

COLTILE = 2560


def project_block(derivs, energy_grads, dirs, width):
    rows = derivs.shape[0]
    steps = (width + COLTILE - 1) // COLTILE
    column = jnp.arange(COLTILE, dtype=jnp.int32)[None, :]
    contract = (((1,), (1,)), ((), ()))

    def advance(index, carry):
        start = index * COLTILE
        keep = column + start < width
        piece = jnp.where(
            keep, lax.dynamic_slice_in_dim(derivs, start, COLTILE, 1), jnp.zeros((), jnp.bfloat16)
        )
        grads = jnp.where(
            keep,
            lax.dynamic_slice_in_dim(energy_grads, start, COLTILE, 1),
            jnp.zeros((), jnp.bfloat16),
        )
        dir_piece = lax.dynamic_slice_in_dim(dirs, start, COLTILE, 1)
        first = carry[0] + lax.dot_general(
            piece, dir_piece, contract, preferred_element_type=jnp.float32
        )
        second = carry[1] + lax.dot_general(
            grads, dir_piece, contract, preferred_element_type=jnp.float32
        )
        return (first, second)

    empty = jnp.zeros((rows, dirs.shape[0]), jnp.float32)
    return lax.fori_loop(0, steps, advance, (empty, empty))


def per_device(derivs, energy_grads, local_energy, directions, widths, live_rows):
    rows = derivs.shape[0]
    proj, projq = project_block(derivs, energy_grads, directions, widths[0])
    live = (jnp.arange(rows, dtype=jnp.int32) < live_rows[0]).astype(jnp.float32)[:, None]
    psum, qsum, count = lax.psum(
        (jnp.sum(proj * live, axis=0), jnp.sum(projq * live, axis=0), jnp.sum(live)), "walk"
    )
    pbar = psum / count
    qbar = qsum / count
    centred = proj - pbar
    pc = (live * centred).astype(jnp.bfloat16)
    hc = (live * (local_energy[:, None] * centred + projq - qbar)).astype(jnp.bfloat16)
    stacked = jnp.stack([hc, pc], axis=0)
    contract = (((0,), (0,)), ((), ()))
    shares = lax.all_to_all(stacked, "blk", split_axis=1, concat_axis=2, tiled=True)
    pshare = shares[1]
    hwhole = lax.dot_general(pshare, shares[0], contract, preferred_element_type=jnp.float32)
    swhole = lax.dot_general(pshare, pshare, contract, preferred_element_type=jnp.float32)
    whole = jnp.stack([hwhole, swhole], axis=0)
    own_rows = lax.psum_scatter(whole, "blk", scatter_dimension=1, tiled=True)
    summed = lax.psum_scatter(own_rows, "walk", scatter_dimension=2, tiled=True)
    summed = summed / count
    return (summed[0], summed[1])


def solution(mesh):
    return jax.shard_map(
        per_device,
        mesh=mesh,
        in_specs=(
            P("walk", "blk"),
            P("walk", "blk"),
            P("walk"),
            P("blk", None),
            P("blk"),
            P("walk"),
        ),
        out_specs=(P("blk", "walk"), P("blk", "walk")),
        check_vma=False,
    )
```

profile of v0, /device:TPU:1, one launch (start us, length us, event | category | flops | bytes accessed | tf_op | source)
XLA Modules:
  0.0 192.5 jit_solution(6123144780549113672)
XLA Ops:
  7.2 0.0 reduce-scatter.5.cloned.1.call-start
  8.5 0.7 fusion.18
  9.2 27.9 %while.13 = (s32[]{:T(128)}, f32[192,32]{0,1:T(8,128)S(1)}, f32[192,32]{0,1:T(8,128)S(1)}, s32[]{:T(128)}, s32[]{:T(128)}, /*index=5*/bf16[192,25600]{1,0:T(8,12...) while((s32[]{:T(128)}, f32[192,32]{0,1:T(8,128)S(1)}, ...), condition=%wide.region_1.2_spmd.clone, body=%wide.region_0.1_spmd.clone.sunk | while | flops 63915012 | bytes 2401963 | solution.py:36
  9.2 0.7 compare_reduce_fusion.2
  9.9 1.6 convolution_add_fusion.5
  11.6 1.6 convolution_add_fusion.4
  13.2 0.7 compare_reduce_fusion.2
  13.9 1.6 convolution_add_fusion.5
  15.6 1.6 convolution_add_fusion.4
  17.2 0.7 compare_reduce_fusion.2
  17.9 1.6 convolution_add_fusion.5
  19.6 1.6 convolution_add_fusion.4
  21.2 0.7 compare_reduce_fusion.2
  21.9 1.6 convolution_add_fusion.5
  23.5 1.6 convolution_add_fusion.4
  25.2 0.7 compare_reduce_fusion.2
  25.9 1.6 convolution_add_fusion.5
  27.5 1.6 convolution_add_fusion.4
  29.2 0.7 compare_reduce_fusion.2
  29.9 1.6 convolution_add_fusion.5
  31.5 1.6 convolution_add_fusion.4
  33.2 0.7 compare_reduce_fusion.2
  33.9 1.6 convolution_add_fusion.5
  35.5 1.6 convolution_add_fusion.4
  37.2 0.1 multiply_reduce_fusion
  37.3 13.7 %all-reduce = (f32[32]{0:T(128)S(1)}, f32[]{:T(128)}, f32[32]{0:T(128)S(1)}) all-reduce(f32[32]{0:T(128)S(1)} %get-tuple-element.73, f32[]{:T(128)} %fusion.18, f32[32]{0:T(128)S(1)} %get-tuple-element.72), channel_id=1, replica_groups=mesh['walk'=8,'blk'=16] {'walk'}, use_global_device_ids=true, to_apply=%region_3.4 | all-reduce | flops 65 | bytes 520 | tf_op jit(solution)/shard_map/psum | solution.py:43
  51.0 0.6 broadcast_divide_fusion.1
  51.6 0.1 fusion.16
  51.7 0.1 copy.18
  51.9 0.1 reshape.30
  52.0 25.9 %all_to_all.15 = bf16[16,2,384]{2,1,0:T(2,128)(2,1)S(1)} all-to-all(bf16[16,2,384]{2,1,0:T(2,128)(2,1)S(1)} %reshape.30), channel_id=1, replica_groups=mesh['walk'=8,'blk'=16] {'blk'}, dimensions={0} | all-to-all | bytes 49152 | tf_op jit(solution)/shard_map/all_to_all | solution.py:53
  77.9 0.1 reshape.31
  78.0 0.1 fusion.19
  78.2 0.1 squeeze.21
  78.3 0.1 squeeze.20
  78.4 0.3 convolution_bitcast_fusion
  78.7 0.3 convolution_bitcast_fusion.1
  79.1 1.5 pad_maximum_fusion
  80.6 0.0 reduce-scatter.5.cloned.1.call-update
  80.6 0.0 reduce-scatter.7.cloned.1.call-start
  80.7 71.8 %reduce-scatter.5.cloned.1.call-done = f32[2,32,512]{2,1,0:T(8,128)} async-done(((f32[2,512,512]{2,1,0:T(8,128)}), f32[2,32,512]{2,1,0:T(8,128)}) %reduce-scatter.5.cloned.1.call-update) | async-done | bytes 131088 | tf_op jit(solution)/shard_map/reduce_scatter | solution.py:58
  152.4 1.1 copy.21
  153.6 1.0 reshape.27
  154.6 28.9 %reduce-scatter.7.cloned.1.call-done = f32[64,64]{1,0:T(8,128)} async-done(((f32[512,64]{1,0:T(8,128)}), f32[64,64]{1,0:T(8,128)}) %reduce-scatter.7.cloned.1.call-update) | async-done | bytes 16400
  183.5 0.9 reshape.28
  184.3 0.1 copy.22
  184.4 0.7 broadcast_divide_fusion
  185.1 0.6 slice_bitcast_fusion
  (9 shorter events, 0.1 us)
Async XLA Ops:
  7.2 145.3 %reduce-scatter.5.cloned.1.call-start = ((), (), s32[]{:S(2)}) async-start(), calls=%async_computation.3 | async-start | bytes 2228224 | tf_op jit(solution)/shard_map/reduce_scatter | solution.py:58
  9.2 42.4 %copy-start = (f32[192]{0:T(256)S(1)}, f32[192]{0:T(256)}, u32[]{:S(2)}) copy-start(f32[192]{0:T(256)} %param.10) | copy-start | bytes 2308
  80.6 102.9 %reduce-scatter.7.cloned.1.call-start = ((), (), s32[]{:S(2)}) async-start(), calls=%async_computation.4 | async-start | bytes 294912
Sparse Core Ops, SparseCore 0:
  80.7 71.6 reduce-scatter.4
  154.9 28.5 reduce-scatter.6
where the time goes:
time: 195 us; the launch traced here: 193 us
  waiting for transfers between devices  101 us (52%)
  blocking collectives  39.6 us (20%)
  matrix products  23.4 us (12%)
  between operations  15.5 us (8%)
  other arithmetic  8.6 us (4%)
  local copies, waits for them, and re-layouts  4.44 us (2%)
    reduce_scatter x1, waiting for transfers between devices, per_device(): own_rows = lax.psum_scatter(whole, 'blk', scatter_dimension=1, tiled=True)  71.8 us
    unnamed x3, waiting for transfers between devices  28.9 us
    all_to_all x1, blocking collectives, per_device(): lax.all_to_all(stacked, 'blk', split_axis=1, concat_axis=2, tiled=True)  25.9 us
    psum x1, blocking collectives, per_device(): lax.psum((jnp.sum(proj * live, axis=0), jnp.sum(projq * live, axis=0), jn...  13.7 us
    dot_general x7, matrix products, advance(): lax.dot_general(piece, dir_piece, contract, preferred_element_type=jnp.fl...  11.4 us
    dot_general x7, matrix products, advance(): lax.dot_general(grads, dir_piece, contract, preferred_element_type=jnp.fl...  11.4 us
    lt x7, other arithmetic, advance(): keep = column + start < width  4.88 us
  transfers between devices with their start and end apart: 2, of which 2 were waited for; matrix products, arithmetic and copies ran while one was open for 0% of the time, Pallas kernels for 0%

commit v1 on v0

v1 whole, which is shorter than its diff:
```python
import functools

import jax
import jax.numpy as jnp
from jax import lax
from jax.experimental import pallas as pl
from jax.experimental.pallas import tpu as pltpu
from jax.sharding import PartitionSpec as P

MESH = pl.DeviceIdType.MESH
F32 = jnp.float32
BF16 = jnp.bfloat16
CHUNK = 64
LANES = 128
SPLIT = 2
AHEAD = 3
NT = (((1,), (1,)), ((), ()))
TN = (((0,), (0,)), ((), ()))


def exact_dot(a, b, dims):
    return lax.dot_general(
        a, b, dims, precision=lax.Precision.HIGHEST, preferred_element_type=F32
    )


def pencil_kernel(
    nw, nb, d_hbm, e_hbm, v_hbm, en_ref, wid_ref, live_ref, o_ref,
    dv, ev, vv, panel, tail, lhs, shift, msg, got,
    dsem, esem, vsem, csend, crecv, asend, arecv, bsend, brecv, msend, mrecv,
):
    w = lax.axis_index("walk")
    b = lax.axis_index("blk")
    rows, cols = d_hbm.shape
    dirs = v_hbm.shape[0]
    width = cols // SPLIT
    chunks = rows // CHUNK
    pieces = [(c, k) for c in range(chunks) for k in range(SPLIT)]

    def dir_copy(k):
        part = (slice(None), pl.ds(k * width, width))
        return pltpu.make_async_copy(v_hbm.at[part], vv.at[part], vsem.at[k])

    def piece_copies(i):
        c, k = pieces[i]
        part = (pl.ds(c * CHUNK, CHUNK), pl.ds(k * width, width))
        return (
            pltpu.make_async_copy(d_hbm.at[part], dv.at[part], dsem.at[i]),
            pltpu.make_async_copy(e_hbm.at[part], ev.at[part], esem.at[i]),
        )

    def start_piece(i):
        if i < SPLIT:
            dir_copy(i).start()
        for copy in piece_copies(i):
            copy.start()

    for i in range(AHEAD):
        start_piece(i)

    walk_peers = [lax.rem(w + r, nw) for r in range(1, nw)]
    blk_peers = [lax.rem(b + r, nb) for r in range(1, nb)]
    barrier = pltpu.get_barrier_semaphore()
    for peer in walk_peers:
        pl.semaphore_signal(barrier, inc=1, device_id=(peer, b), device_id_type=MESH)
    for peer in blk_peers:
        pl.semaphore_signal(barrier, inc=1, device_id=(w, peer), device_id_type=MESH)

    lane = lax.broadcasted_iota(jnp.int32, (1, LANES), 1)
    low = lane < CHUNK
    used = wid_ref[0]
    live_rows = live_ref[0]

    def project(c):
        total = None
        for k in range(SPLIT):
            i = c * SPLIT + k
            span = pl.ds(k * width, width)
            if c == 0:
                dir_copy(k).wait()
                column = lax.broadcasted_iota(jnp.int32, (dirs, width), 1) + k * width
                vv[:, span] = jnp.where(
                    column < used, vv[:, span].astype(F32), 0.0
                ).astype(BF16)
            for copy in piece_copies(i):
                copy.wait()
            if i + AHEAD < len(pieces):
                start_piece(i + AHEAD)
            rs = pl.ds(c * CHUNK, CHUNK)
            weights = vv[:, span]
            part = jnp.concatenate(
                [
                    lax.dot_general(weights, dv[rs, span], NT, preferred_element_type=F32),
                    lax.dot_general(weights, ev[rs, span], NT, preferred_element_type=F32),
                ],
                axis=1,
            )
            total = part if total is None else total + part
        return total

    row8 = lax.broadcasted_iota(jnp.int32, (8, LANES), 0)
    lane8 = lax.broadcasted_iota(jnp.int32, (8, LANES), 1)
    first_low = jnp.where((row8 == 0) & (lane8 < CHUNK), 1.0, 0.0)
    first_high = jnp.where((row8 == 0) & (lane8 >= CHUNK), 1.0, 0.0)
    halves = first_low + jnp.where((row8 == 1) & (lane8 >= CHUNK), 1.0, 0.0)

    def energies(c):
        lo = (c * CHUNK) // LANES * LANES
        if c % 2 == 0 and lo + LANES > rows:
            e = jnp.concatenate(
                [en_ref[:, lo:rows], jnp.zeros((1, LANES - (rows - lo)), F32)], axis=1
            )
        else:
            e = en_ref[:, lo : lo + LANES]
        if c % 2:
            e = pltpu.roll(e, CHUNK, 1)
        walker = c * CHUNK + lane
        return jnp.where(low & (walker < live_rows), e, 0.0)

    def panels(c, s, common):
        walker = c * CHUNK + jnp.where(low, lane, lane - CHUNK)
        d = jnp.where(walker < live_rows, s - common, 0.0)
        erow = energies(c)
        g = (d + pltpu.roll(d * erow, CHUNK, 1)).astype(BF16)
        own = jnp.where(low, g.astype(F32), 0.0)
        lhs[c] = jnp.concatenate(
            [own, first_low, pltpu.roll(own, CHUNK, 1), first_high], axis=0
        ).astype(BF16)
        probe = jnp.where(row8 == 1, erow, first_low)
        return g, exact_dot(probe, own, NT), erow

    s0 = project(0)
    pl.semaphore_wait(barrier, nw - 1 + nb - 1)

    mean = exact_dot(halves * (1.0 / CHUNK), s0, NT)
    shift[w] = jnp.concatenate([mean, jnp.zeros((8, LANES - dirs), F32)], axis=1)
    for peer in walk_peers:
        pltpu.make_async_remote_copy(
            src_ref=shift.at[w], dst_ref=shift.at[w], send_sem=csend, recv_sem=crecv,
            device_id=(peer, b), device_id_type=MESH,
        ).start()

    s1 = project(1)
    others = pl.ds(0, nw - 1)
    pltpu.make_async_copy(shift.at[others], shift.at[others], crecv).wait()
    common = shift[0]
    for i in range(1, nw):
        common = common + shift[i]
    common = exact_dot(common[:, :dirs] * (1.0 / nw), halves, TN)

    g0, rv0, e0 = panels(0, s0, common)
    g1, rv1, e1 = panels(1, s1, common)
    panel[b, 0] = g0
    panel[b, 1] = g1
    for peer in blk_peers:
        pltpu.make_async_remote_copy(
            src_ref=panel.at[b], dst_ref=panel.at[b], send_sem=asend, recv_sem=arecv,
            device_id=(w, peer), device_id_type=MESH,
        ).start()

    s2 = project(2)
    g2, rv2, e2 = panels(2, s2, common)
    tail[b] = g2
    for peer in blk_peers:
        pltpu.make_async_remote_copy(
            src_ref=tail.at[b], dst_ref=tail.at[b], send_sem=bsend, recv_sem=brecv,
            device_id=(w, peer), device_id_type=MESH,
        ).start()

    rv = rv0 + rv1 + rv2
    esum = jnp.sum(e0 + e1 + e2, axis=1, keepdims=True)
    rv = jnp.concatenate([rv, jnp.zeros((8, LANES - dirs), F32)], axis=1)
    small = jnp.where(
        row8 == 1,
        rv[0:1, :],
        jnp.where(
            row8 == 2,
            rv[1:2, :],
            jnp.where(row8 == 3, esum, jnp.where(row8 == 4, live_rows.astype(F32), 0.0)),
        ),
    )

    pair = pl.ds(0, nb - 1)
    pltpu.make_async_copy(panel.at[pair], panel.at[pair], arecv).wait()
    gram = lax.dot_general(
        lhs[0], panel[:, 0].reshape(nb * dirs, LANES), NT, preferred_element_type=F32
    ) + lax.dot_general(
        lhs[1], panel[:, 1].reshape(nb * dirs, LANES), NT, preferred_element_type=F32
    )
    pltpu.make_async_copy(tail.at[pair], tail.at[pair], brecv).wait()
    gram = gram + lax.dot_general(
        lhs[2], tail[...].reshape(nb * dirs, LANES), NT, preferred_element_type=F32
    )
    high = dirs + 8
    extra = jnp.concatenate([jnp.zeros((dirs, LANES), F32), small], axis=0)
    for t in range(nb * dirs // LANES):
        tile = gram[:, t * LANES : (t + 1) * LANES]
        cpart, hpart = tile[:high], tile[high:]
        msg[2 * t] = jnp.where(low, cpart, pltpu.roll(hpart, CHUNK, 1)) + extra
        msg[2 * t + 1] = jnp.where(low, pltpu.roll(cpart, CHUNK, 1), hpart) + extra
    for peer in walk_peers:
        pltpu.make_async_remote_copy(
            src_ref=msg.at[peer], dst_ref=got.at[w], send_sem=msend, recv_sem=mrecv,
            device_id=(peer, b), device_id_type=MESH,
        ).start()
    got[w] = msg[w]

    pltpu.make_async_copy(shift.at[others], shift.at[others], csend).wait()
    pltpu.make_async_copy(panel.at[pair], panel.at[pair], asend).wait()
    pltpu.make_async_copy(tail.at[pair], tail.at[pair], bsend).wait()
    pltpu.make_async_copy(got.at[others], got.at[others], mrecv).wait()

    total = got[0]
    for i in range(1, nw):
        total = total + got[i]
    jsum = total[dirs : dirs + 1]
    isum = total[dirs + 1 : dirs + 2, :dirs]
    usum = total[dirs + 2 : dirs + 3, :dirs]
    esum = total[dirs + 3 : dirs + 4]
    inv = 1.0 / total[dirs + 4 : dirs + 5]
    di = isum * inv[:, :dirs]
    wi = usum - di * esum[:, :dirs]
    dj = jnp.where(low, 0.0, pltpu.roll(jsum * inv, CHUNK, 1))
    left = jnp.where(row8[:, :dirs] == 0, di, jnp.where(row8[:, :dirs] == 1, wi, 0.0))
    right = jnp.where(row8 == 0, jsum, jnp.where(row8 == 1, dj, 0.0))
    o_ref[...] = (total[:dirs] - exact_dot(left, right, TN)) * inv
    pltpu.make_async_copy(got.at[others], got.at[others], msend).wait()


def solution(mesh):
    nw, nb = mesh.shape["walk"], mesh.shape["blk"]

    def per_device(derivs, energy_grads, local_energy, directions, widths, live_rows):
        rows, cols = derivs.shape
        dirs = directions.shape[0]
        chunks = rows // CHUNK
        any_spec = pl.BlockSpec(memory_space=pl.ANY)
        smem_spec = pl.BlockSpec(memory_space=pltpu.SMEM)
        vmem_spec = pl.BlockSpec(memory_space=pltpu.VMEM)
        dma = pltpu.SemaphoreType.DMA
        out = pl.pallas_call(
            functools.partial(pencil_kernel, nw, nb),
            out_shape=jax.ShapeDtypeStruct((dirs, LANES), F32),
            in_specs=[any_spec, any_spec, any_spec, vmem_spec, smem_spec, smem_spec],
            out_specs=vmem_spec,
            scratch_shapes=[
                pltpu.VMEM((rows, cols), BF16),
                pltpu.VMEM((rows, cols), BF16),
                pltpu.VMEM((dirs, cols), BF16),
                pltpu.VMEM((nb, 2, dirs, LANES), BF16),
                pltpu.VMEM((nb, dirs, LANES), BF16),
                pltpu.VMEM((chunks, 2 * (dirs + 8), LANES), BF16),
                pltpu.VMEM((nw, 8, LANES), F32),
                pltpu.VMEM((nw, dirs + 8, LANES), F32),
                pltpu.VMEM((nw, dirs + 8, LANES), F32),
                dma((chunks * SPLIT,)),
                dma((chunks * SPLIT,)),
                dma((SPLIT,)),
            ]
            + [dma(())] * 8,
            compiler_params=pltpu.CompilerParams(
                collective_id=0, has_side_effects=True, vmem_limit_bytes=48 << 20
            ),
            name="pencil",
        )(
            derivs, energy_grads, directions, local_energy.reshape(1, rows), widths, live_rows
        )
        return out[:, CHUNK:], out[:, :CHUNK]

    return jax.shard_map(
        per_device,
        mesh=mesh,
        in_specs=(
            P("walk", "blk"), P("walk", "blk"), P("walk"), P("blk", None), P("blk"), P("walk"),
        ),
        out_specs=(P("blk", "walk"), P("blk", "walk")),
        check_vma=False,
    )
```

time: 195 us -> 31.3 us (0.16); the launches traced: 193 us -> 31.1 us
  waiting for transfers between devices: 101 us -> 0 us
  blocking collectives: 39.6 us -> 0 us
  Pallas kernels: 0 us -> 26.4 us
  matrix products: 23.4 us -> 0 us
  between operations: 15.5 us -> 1.94 us
  other arithmetic: 8.6 us -> 0 us
    reduce_scatter x1 -> x0, waiting for transfers between devices: 71.8 us -> none  [per_device(): own_rows = lax.psum_scatter(whole, 'blk', scatter_dimension=1, tiled=True)]
    unnamed x3 -> x0, waiting for transfers between devices: 28.9 us -> none
    pallas_call x0 -> x1, Pallas kernels: none -> 26.4 us  [per_device(): pl.pallas_call(functools.partial(pencil_kernel, nw, nb), out_shape=jax.Sh...]
    all_to_all x1 -> x0, blocking collectives: 25.9 us -> none  [per_device(): lax.all_to_all(stacked, 'blk', split_axis=1, concat_axis=2, tiled=True)]
    dot_general x16 -> x0, matrix products: 23.4 us -> none  [the longest x7 11.4 us: advance(): lax.dot_general(piece, dir_piece, contract, preferred_element_type=jnp.fl...]
    psum x1 -> x0, blocking collectives: 13.7 us -> none  [per_device(): lax.psum((jnp.sum(proj * live, axis=0), jnp.sum(projq * live, axis=0), jn...]
    lt x7 -> x0, other arithmetic: 4.88 us -> none  [advance(): keep = column + start < width]
  transfers between devices with their start and end apart: 2 -> 0, of which waited for: 2 -> 0; matrix products, arithmetic and copies ran while one was open for 0% -> 0% of each run, Pallas kernels for 0% -> 0%
where the time goes in v1:
time: 31.3 us; the launch traced here: 31.1 us
  Pallas kernels  26.4 us (84%)
  local copies, waits for them, and re-layouts  2.78 us (9%)
  between operations  1.94 us (6%)
    pallas_call x1, Pallas kernels, per_device(): pl.pallas_call(functools.partial(pencil_kernel, nw, nb), out_shape=jax.Sh...  26.4 us
    unnamed x4, local copies, waits for them, and re-layouts  2.1 us
    slice x1, local copies, waits for them, and re-layouts, per_device(): return (out[:, CHUNK:], out[:, :CHUNK])  0.68 us

profile of v1, /device:TPU:1, one launch (start us, length us, event | category | flops | bytes accessed | tf_op | source)
XLA Modules:
  0.0 31.1 jit_solution(17615315001179537125)
XLA Ops:
  1.9 0.0 copy-start
  1.9 1.4 %copy-done = bf16[32,25600]{1,0:T(8,128)(2,1)S(1)} copy-done((bf16[32,25600]{1,0:T(8,128)(2,1)S(1)}, bf16[32,25600]{1,0:T(8,128)(2,1)}, u32[]{:S(2)}) %copy-start) | copy-done | bytes 1638424
  3.4 0.0 copy-start.1
  3.4 0.7 %copy-done.1 = f32[192]{0:T(256)S(1)} copy-done((f32[192]{0:T(256)S(1)}, f32[192]{0:T(256)}, u32[]{:S(2)}) %copy-start.1) | copy-done | bytes 792
  4.0 26.4 %pencil.1 = f32[32,128]{1,0:T(8,128)S(1)} custom-call(bf16[192,25600]{1,0:T(8,128)(2,1)} %d_hbm.1, bf16[192,25600]{1,0:T(8,128)(2,1)} %e_hbm.1, bf16[32,25600]{1,0:T(8,128)(2,1)S(1)} %copy-done, f32[1,192]{1,0:T(1,128)S(1)} %bitcast.1, s32[1]{0:T(128)S(6)} %copy.8.wid_ref, s32[1]{0:T(128)S(6)} %copy.9.live_ref), custom_call_target="tpu_custom_call" | custom-call | tf_op jit(solution)/shard_map/pencil/pallas_call | solution.py:241
  30.4 0.7 %fusion = (f32[32,64]{1,0:T(8,128)}, f32[32,64]{1,0:T(8,128)}) fusion(f32[32,128]{1,0:T(8,128)S(1)} %pencil.1), kind=kLoop, calls=%fused_computation | loop fusion | bytes 32768 | tf_op jit(solution)/shard_map/slice | solution.py:268
Async XLA Ops:
  1.9 1.4 %copy-start = (bf16[32,25600]{1,0:T(8,128)(2,1)S(1)}, bf16[32,25600]{1,0:T(8,128)(2,1)}, u32[]{:S(2)}) copy-start(bf16[32,25600]{1,0:T(8,128)(2,1)} %v_hbm.1) | copy-start | bytes 4915204
  3.4 0.7 %copy-start.1 = (f32[192]{0:T(256)S(1)}, f32[192]{0:T(256)}, u32[]{:S(2)}) copy-start(f32[192]{0:T(256)} %param.8) | copy-start | bytes 2308

commit v2 on v1

v2 whole, which is shorter than its diff:
```python
import functools

import jax
import jax.numpy as jnp
from jax import lax
from jax.experimental import pallas as pl
from jax.experimental.pallas import tpu as pltpu
from jax.sharding import PartitionSpec as P

MESH = pl.DeviceIdType.MESH
F32 = jnp.float32
BF16 = jnp.bfloat16
CHUNK = 64
LANES = 128
SPLIT = 2
AHEAD = 3
EARLY = 2
NT = (((1,), (1,)), ((), ()))
TN = (((0,), (0,)), ((), ()))


def exact_dot(a, b, dims):
    return lax.dot_general(
        a, b, dims, precision=lax.Precision.HIGHEST, preferred_element_type=F32
    )


def two_terms(x):
    hi = x.astype(BF16).astype(F32)
    return hi, (x - hi).astype(BF16).astype(F32)


def ring_peers(me, count, inner):
    outer = count // inner
    hops = lambda n, size: min(n, size - n)
    steps = [(i, j) for i in range(outer) for j in range(inner) if (i, j) != (0, 0)]
    steps.sort(key=lambda s: -(hops(s[0], outer) + hops(s[1], inner)))
    major, minor = me // inner, lax.rem(me, inner)
    return [
        lax.rem(major + i, outer) * inner + lax.rem(minor + j, inner) for i, j in steps
    ]


def pencil_kernel(
    nw, nb, d_hbm, e_hbm, v_hbm, en_hbm, wid_ref, live_ref, o_ref,
    dv, ev, vv, en_ref, panel, tail, lhs, msg, got, vecs,
    dsem, esem, vsem, ensem, asend, arecv, bsend, brecv, msend, mrecv,
):
    w = lax.axis_index("walk")
    b = lax.axis_index("blk")
    rows, cols = d_hbm.shape
    dirs = v_hbm.shape[0]
    width = cols // SPLIT
    chunks = rows // CHUNK
    pieces = [(c, k) for c in range(chunks) for k in range(SPLIT)]

    def dir_copy(k):
        part = (slice(None), pl.ds(k * width, width))
        return pltpu.make_async_copy(v_hbm.at[part], vv.at[part], vsem.at[k])

    def piece_copies(i):
        c, k = pieces[i]
        part = (pl.ds(c * CHUNK, CHUNK), pl.ds(k * width, width))
        return (
            pltpu.make_async_copy(d_hbm.at[part], dv.at[part], dsem.at[i]),
            pltpu.make_async_copy(e_hbm.at[part], ev.at[part], esem.at[i]),
        )

    def start_piece(i):
        if i < SPLIT:
            dir_copy(i).start()
        for copy in piece_copies(i):
            copy.start()

    en_copy = pltpu.make_async_copy(en_hbm, en_ref, ensem)
    for i in range(AHEAD):
        start_piece(i)
    en_copy.start()

    walk_peers = ring_peers(w, nw, 2)
    blk_peers = ring_peers(b, nb, 4)
    barrier = pltpu.get_barrier_semaphore()
    for peer in blk_peers:
        pl.semaphore_signal(barrier, inc=1, device_id=(w, peer), device_id_type=MESH)
    for peer in walk_peers:
        pl.semaphore_signal(barrier, inc=1, device_id=(peer, b), device_id_type=MESH)

    lane = lax.broadcasted_iota(jnp.int32, (1, LANES), 1)
    low = lane < CHUNK
    used = wid_ref[0]
    live_rows = live_ref[0]

    def project(c):
        total = None
        for k in range(SPLIT):
            i = c * SPLIT + k
            span = pl.ds(k * width, width)
            if c == 0:
                dir_copy(k).wait()
                column = lax.broadcasted_iota(jnp.int32, (dirs, width), 1) + k * width
                vv[:, span] = jnp.where(
                    column < used, vv[:, span].astype(F32), 0.0
                ).astype(BF16)
            for copy in piece_copies(i):
                copy.wait()
            if i + AHEAD < len(pieces):
                start_piece(i + AHEAD)
            rs = pl.ds(c * CHUNK, CHUNK)
            weights = vv[:, span]
            part = jnp.concatenate(
                [
                    lax.dot_general(weights, dv[rs, span], NT, preferred_element_type=F32),
                    lax.dot_general(weights, ev[rs, span], NT, preferred_element_type=F32),
                ],
                axis=1,
            )
            total = part if total is None else total + part
        return total

    row8 = lax.broadcasted_iota(jnp.int32, (8, LANES), 0)
    lane8 = lax.broadcasted_iota(jnp.int32, (8, LANES), 1)

    def mark(row, lo, hi):
        return jnp.where((row8 == row) & (lane8 >= lo) & (lane8 < hi), 1.0, 0.0)

    first_low = mark(0, 0, CHUNK)
    first_high = mark(0, CHUNK, LANES)
    blank = jnp.zeros((dirs, LANES), F32)
    tall = 2 * dirs + 8

    def energies(c):
        lo = (c * CHUNK) // LANES * LANES
        if lo + LANES > rows:
            e = jnp.concatenate(
                [en_ref[:, lo:rows], jnp.zeros((1, LANES - (rows - lo)), F32)], axis=1
            )
        else:
            e = en_ref[:, lo : lo + LANES]
        if c % 2:
            e = pltpu.roll(e, CHUNK, 1)
        return jnp.where(low & (c * CHUNK + lane < live_rows), e, 0.0)

    def panels(c, s, common):
        walker = c * CHUNK + jnp.where(low, lane, lane - CHUNK)
        d = jnp.where(walker < live_rows, s - common, 0.0)
        erow = energies(c)
        return d, erow, (d + pltpu.roll(d * erow, CHUNK, 1)).astype(BF16)

    def own_side(c, d, erow):
        own = jnp.where(low, d, 0.0)
        hi, lo = two_terms(own)
        lhs[c] = jnp.concatenate(
            [
                hi, lo, first_low,
                pltpu.roll(hi, CHUNK, 1), pltpu.roll(lo, CHUNK, 1), first_high,
            ],
            axis=0,
        ).astype(BF16)
        return exact_dot(jnp.where(row8 == 3, erow, mark(2, 0, CHUNK)), own, NT)

    def send_all(src, dst, send_sem, recv_sem):
        for peer in blk_peers:
            pltpu.make_async_remote_copy(
                src_ref=src, dst_ref=dst, send_sem=send_sem, recv_sem=recv_sem,
                device_id=(w, peer), device_id_type=MESH,
            ).start()

    s0 = project(0)
    pmean = jnp.sum(jnp.where(low, s0, 0.0), axis=1, keepdims=True) * (1.0 / CHUNK)
    qmean = jnp.sum(jnp.where(low, 0.0, s0), axis=1, keepdims=True) * (1.0 / CHUNK)
    phi, plo = two_terms(pmean)
    qhi, qlo = two_terms(qmean)
    common = jnp.where(low, phi + plo, qhi + qlo)
    shift = jnp.where(
        lane == 0, phi, jnp.where(lane == 1, plo, jnp.where(lane == 2, qhi, jnp.where(lane == 3, qlo, 0.0)))
    )
    s1 = project(1)
    en_copy.wait()
    d0, e0, g0 = panels(0, s0, common)
    d1, e1, g1 = panels(1, s1, common)
    panel[b, 0] = g0
    panel[b, 1] = g1
    panel[b, 2] = shift.astype(BF16)
    pl.semaphore_wait(barrier, nw - 1 + nb - 1)
    send_all(panel.at[b], panel.at[b], asend, arecv)

    s2 = project(2)
    d2, e2, g2 = panels(2, s2, common)
    tail[b] = g2
    send_all(tail.at[b], tail.at[b], bsend, brecv)

    lhs[chunks] = jnp.concatenate(
        [blank, blank, mark(1, 0, 2), blank, blank, mark(1, 2, 4)], axis=0
    ).astype(BF16)
    rv = own_side(0, d0, e0) + own_side(1, d1, e1) + own_side(2, d2, e2)
    rv = rv + exact_dot(mark(4, 0, 2), shift, NT)
    rv = jnp.concatenate([rv, jnp.zeros((8, LANES - dirs), F32)], axis=1)
    esum = jnp.sum(e0 + e1 + e2, axis=1, keepdims=True)
    small = rv + jnp.where(
        row8 == 5, esum, jnp.where(row8 == 6, live_rows.astype(F32), 0.0)
    )

    def gram_of(c, block):
        return lax.dot_general(
            lhs[c], block.reshape(nb * dirs, LANES), NT, preferred_element_type=F32
        )

    others = pl.ds(0, nb - 1)
    pltpu.make_async_copy(panel.at[others], panel.at[others], arecv).wait()
    gram = gram_of(0, panel[:, 0]) + gram_of(1, panel[:, 1]) + gram_of(chunks, panel[:, 2])
    pltpu.make_async_copy(tail.at[others], tail.at[others], brecv).wait()
    gram = gram + gram_of(2, tail[...])

    for t in range(nb * dirs // LANES):
        tile = gram[:, t * LANES : (t + 1) * LANES]
        sums = []
        for part in (tile[:tall], tile[tall:]):
            sums.append(
                jnp.concatenate([part[:dirs] + part[dirs : 2 * dirs], part[2 * dirs :]], axis=0)
            )
        cpart, hpart = sums
        for i, both in enumerate(
            (
                jnp.where(low, cpart, pltpu.roll(hpart, CHUNK, 1)),
                jnp.where(low, pltpu.roll(cpart, CHUNK, 1), hpart),
            )
        ):
            hi, lo = two_terms(both[dirs:] + small)
            msg[2 * t + i] = jnp.concatenate([both[:dirs], hi, lo], axis=0).astype(BF16)
    for peer in walk_peers:
        pltpu.make_async_remote_copy(
            src_ref=msg.at[peer], dst_ref=got.at[w], send_sem=msend, recv_sem=mrecv,
            device_id=(peer, b), device_id_type=MESH,
        ).start()
    got[w] = msg[w]

    pltpu.make_async_copy(panel.at[others], panel.at[others], asend).wait()
    pltpu.make_async_copy(tail.at[others], tail.at[others], bsend).wait()
    groups = pl.ds(0, nw - 1)
    pltpu.make_async_copy(got.at[groups], got.at[groups], mrecv).wait()

    total = jnp.zeros((dirs, LANES), F32)
    for i in range(nw):
        one = got[i].astype(F32)
        total = total + one[:dirs]
        vecs[i] = one[dirs : dirs + 8] + one[dirs + 8 :]
    jsum, jshift = vecs[:, 0], vecs[:, 1]
    isum, usum, ishift = vecs[:, 2, :dirs], vecs[:, 3, :dirs], vecs[:, 4, :dirs]
    esum, live = vecs[:, 5], vecs[:, 6]
    inv = 1.0 / jnp.sum(live, axis=0, keepdims=True)
    jref = jnp.sum(jnp.where(low, jsum, 0.0) + live * jshift, axis=0, keepdims=True) * inv
    iref = (
        jnp.sum(isum + live[:, :dirs] * ishift, axis=0, keepdims=True) * inv[:, :dirs]
    )
    jdiff = jshift - jref
    pdiff = jnp.where(low, 0.0, pltpu.roll(jdiff, CHUNK, 1))
    left = jnp.concatenate([usum, isum, ishift - iref], axis=0)
    right = jnp.concatenate([pdiff, jdiff, jsum + live * jdiff + esum * pdiff], axis=0)
    o_ref[...] = (total + exact_dot(left, right, TN)) * inv
    pltpu.make_async_copy(got.at[groups], got.at[groups], msend).wait()


def solution(mesh):
    nw, nb = mesh.shape["walk"], mesh.shape["blk"]

    def per_device(derivs, energy_grads, local_energy, directions, widths, live_rows):
        rows, cols = derivs.shape
        dirs = directions.shape[0]
        chunks = rows // CHUNK
        hbm_spec = pl.BlockSpec(memory_space=pltpu.HBM)
        smem_spec = pl.BlockSpec(memory_space=pltpu.SMEM)
        dma = pltpu.SemaphoreType.DMA
        out = pl.pallas_call(
            functools.partial(pencil_kernel, nw, nb),
            out_shape=jax.ShapeDtypeStruct((dirs, LANES), F32),
            in_specs=[hbm_spec] * 4 + [smem_spec] * 2,
            out_specs=pl.BlockSpec(memory_space=pltpu.VMEM),
            scratch_shapes=[
                pltpu.VMEM((rows, cols), BF16),
                pltpu.VMEM((rows, cols), BF16),
                pltpu.VMEM((dirs, cols), BF16),
                pltpu.VMEM((1, rows), F32),
                pltpu.VMEM((nb, EARLY + 1, dirs, LANES), BF16),
                pltpu.VMEM((nb, dirs, LANES), BF16),
                pltpu.VMEM((chunks + 1, 4 * dirs + 16, LANES), BF16),
                pltpu.VMEM((nw, dirs + 16, LANES), BF16),
                pltpu.VMEM((nw, dirs + 16, LANES), BF16),
                pltpu.VMEM((nw, 8, LANES), F32),
                dma((chunks * SPLIT,)),
                dma((chunks * SPLIT,)),
                dma((SPLIT,)),
            ]
            + [dma(())] * 7,
            compiler_params=pltpu.CompilerParams(
                collective_id=0, has_side_effects=True, vmem_limit_bytes=53 << 20
            ),
            name="pencil",
        )(
            derivs, energy_grads, directions, local_energy.reshape(1, rows), widths, live_rows
        )
        return out[:, CHUNK:], out[:, :CHUNK]

    return jax.shard_map(
        per_device,
        mesh=mesh,
        in_specs=(
            P("walk", "blk"), P("walk", "blk"), P("walk"), P("blk", None), P("blk"), P("walk"),
        ),
        out_specs=(P("blk", "walk"), P("blk", "walk")),
        check_vma=False,
    )
```

time: 31.3 us -> 29.2 us (0.933)
  local copies, waits for them, and re-layouts: 2.78 us -> 1.35 us
  Pallas kernels: 26.4 us -> 25.8 us
    unnamed x4 -> x2, local copies, waits for them, and re-layouts: 2.1 us -> 0.67 us
    pallas_call x1, Pallas kernels: 26.4 us -> 25.8 us  [per_device(): pl.pallas_call(functools.partial(pencil_kernel, nw, nb), out_shape=jax.Sh...]
where the time goes in v2:
time: 29.2 us; the launch traced here: 29.1 us
  Pallas kernels  25.8 us (88%)
  between operations  1.94 us (7%)
  local copies, waits for them, and re-layouts  1.35 us (5%)
    pallas_call x1, Pallas kernels, per_device(): pl.pallas_call(functools.partial(pencil_kernel, nw, nb), out_shape=jax.Sh...  25.8 us
    slice x1, local copies, waits for them, and re-layouts, per_device(): return (out[:, CHUNK:], out[:, :CHUNK])  0.68 us
    unnamed x2, local copies, waits for them, and re-layouts  0.67 us

profile of v2, /device:TPU:1, one launch (start us, length us, event | category | flops | bytes accessed | tf_op | source)
XLA Modules:
  0.0 29.1 jit_solution(10435737930890682027)
XLA Ops:
  1.9 0.0 copy-start
  1.9 0.7 %copy-done = f32[192]{0:T(256)S(1)} copy-done((f32[192]{0:T(256)S(1)}, f32[192]{0:T(256)}, u32[]{:S(2)}) %copy-start) | copy-done | bytes 792
  2.6 25.8 %pencil.1 = f32[32,128]{1,0:T(8,128)S(1)} custom-call(bf16[192,25600]{1,0:T(8,128)(2,1)} %d_hbm.1, bf16[192,25600]{1,0:T(8,128)(2,1)} %e_hbm.1, bf16[32,25600]{1,0:T(8,128)(2,1)} %v_hbm.1, f32[1,192]{1,0:T(1,128)S(1)} %bitcast.1, s32[1]{0:T(128)S(6)} %copy.8.wid_ref, s32[1]{0:T(128)S(6)} %copy.9.live_ref), custom_call_target="tpu_custom_call" | custom-call | tf_op jit(solution)/shard_map/pencil/pallas_call | solution.py:273
  28.4 0.7 %fusion = (f32[32,64]{1,0:T(8,128)}, f32[32,64]{1,0:T(8,128)}) fusion(f32[32,128]{1,0:T(8,128)S(1)} %pencil.1), kind=kLoop, calls=%fused_computation | loop fusion | bytes 32768 | tf_op jit(solution)/shard_map/slice | solution.py:301
Async XLA Ops:
  1.9 0.7 %copy-start = (f32[192]{0:T(256)S(1)}, f32[192]{0:T(256)}, u32[]{:S(2)}) copy-start(f32[192]{0:T(256)} %param.8) | copy-start | bytes 2308

commit v3 on v2

--- a/solution.py
+++ b/solution.py
@@ -14,7 +14,6 @@
 LANES = 128
 SPLIT = 2
 AHEAD = 3
-EARLY = 2
 NT = (((1,), (1,)), ((), ()))
 TN = (((0,), (0,)), ((), ()))
 
@@ -43,8 +42,8 @@
 
 def pencil_kernel(
     nw, nb, d_hbm, e_hbm, v_hbm, en_hbm, wid_ref, live_ref, o_ref,
-    dv, ev, vv, en_ref, panel, tail, lhs, msg, got, vecs,
-    dsem, esem, vsem, ensem, asend, arecv, bsend, brecv, msend, mrecv,
+    dv, ev, vv, en_ref, panel, middle, tail, lhs, base, msg, got, vecs,
+    dsem, esem, vsem, brecv, ensem, asend, arecv, csend, crecv, bsend, msend, mrecv,
 ):
     w = lax.axis_index("walk")
     b = lax.axis_index("blk")
@@ -54,8 +53,10 @@
     chunks = rows // CHUNK
     pieces = [(c, k) for c in range(chunks) for k in range(SPLIT)]
 
+    quarter = width // 2
+
     def dir_copy(k):
-        part = (slice(None), pl.ds(k * width, width))
+        part = (slice(None), pl.ds(k * quarter, quarter))
         return pltpu.make_async_copy(v_hbm.at[part], vv.at[part], vsem.at[k])
 
     def piece_copies(i):
@@ -68,7 +69,8 @@
 
     def start_piece(i):
         if i < SPLIT:
-            dir_copy(i).start()
+            dir_copy(2 * i).start()
+            dir_copy(2 * i + 1).start()
         for copy in piece_copies(i):
             copy.start()
 
@@ -96,11 +98,11 @@
             i = c * SPLIT + k
             span = pl.ds(k * width, width)
             if c == 0:
-                dir_copy(k).wait()
-                column = lax.broadcasted_iota(jnp.int32, (dirs, width), 1) + k * width
-                vv[:, span] = jnp.where(
-                    column < used, vv[:, span].astype(F32), 0.0
-                ).astype(BF16)
+                for q in (2 * k, 2 * k + 1):
+                    dir_copy(q).wait()
+                    part = pl.ds(q * quarter, quarter)
+                    column = lax.broadcasted_iota(jnp.int32, (1, quarter), 1) + q * quarter
+                    vv[:, part] = vv[:, part] * jnp.where(column < used, 1.0, 0.0).astype(BF16)
             for copy in piece_copies(i):
                 copy.wait()
             if i + AHEAD < len(pieces):
@@ -158,10 +160,10 @@
         ).astype(BF16)
         return exact_dot(jnp.where(row8 == 3, erow, mark(2, 0, CHUNK)), own, NT)
 
-    def send_all(src, dst, send_sem, recv_sem):
+    def send_all(buf, send_sem, recv_sem):
         for peer in blk_peers:
             pltpu.make_async_remote_copy(
-                src_ref=src, dst_ref=dst, send_sem=send_sem, recv_sem=recv_sem,
+                src_ref=buf.at[b], dst_ref=buf.at[b], send_sem=send_sem, recv_sem=recv_sem,
                 device_id=(w, peer), device_id_type=MESH,
             ).start()
 
@@ -174,20 +176,20 @@
     shift = jnp.where(
         lane == 0, phi, jnp.where(lane == 1, plo, jnp.where(lane == 2, qhi, jnp.where(lane == 3, qlo, 0.0)))
     )
-    s1 = project(1)
     en_copy.wait()
     d0, e0, g0 = panels(0, s0, common)
-    d1, e1, g1 = panels(1, s1, common)
     panel[b, 0] = g0
-    panel[b, 1] = g1
-    panel[b, 2] = shift.astype(BF16)
+    panel[b, 1] = shift.astype(BF16)
     pl.semaphore_wait(barrier, nw - 1 + nb - 1)
-    send_all(panel.at[b], panel.at[b], asend, arecv)
-
-    s2 = project(2)
-    d2, e2, g2 = panels(2, s2, common)
+    send_all(panel, asend, arecv)
+
+    d1, e1, g1 = panels(1, project(1), common)
+    middle[b] = g1
+    send_all(middle, csend, crecv)
+
+    d2, e2, g2 = panels(2, project(2), common)
     tail[b] = g2
-    send_all(tail.at[b], tail.at[b], bsend, brecv)
+    send_all(tail, bsend, brecv.at[b])
 
     lhs[chunks] = jnp.concatenate(
         [blank, blank, mark(1, 0, 2), blank, blank, mark(1, 2, 4)], axis=0
@@ -200,41 +202,56 @@
         row8 == 5, esum, jnp.where(row8 == 6, live_rows.astype(F32), 0.0)
     )
 
-    def gram_of(c, block):
+    def gram_of(c, block, count):
         return lax.dot_general(
-            lhs[c], block.reshape(nb * dirs, LANES), NT, preferred_element_type=F32
+            lhs[c], block.reshape(count * dirs, LANES), NT, preferred_element_type=F32
         )
+
+    def halves_of(tile):
+        return [
+            jnp.concatenate([part[:dirs] + part[dirs : 2 * dirs], part[2 * dirs :]], axis=0)
+            for part in (tile[:tall], tile[tall:])
+        ]
 
     others = pl.ds(0, nb - 1)
     pltpu.make_async_copy(panel.at[others], panel.at[others], arecv).wait()
-    gram = gram_of(0, panel[:, 0]) + gram_of(1, panel[:, 1]) + gram_of(chunks, panel[:, 2])
-    pltpu.make_async_copy(tail.at[others], tail.at[others], brecv).wait()
-    gram = gram + gram_of(2, tail[...])
-
-    for t in range(nb * dirs // LANES):
-        tile = gram[:, t * LANES : (t + 1) * LANES]
-        sums = []
-        for part in (tile[:tall], tile[tall:]):
-            sums.append(
-                jnp.concatenate([part[:dirs] + part[dirs : 2 * dirs], part[2 * dirs :]], axis=0)
-            )
-        cpart, hpart = sums
-        for i, both in enumerate(
-            (
-                jnp.where(low, cpart, pltpu.roll(hpart, CHUNK, 1)),
-                jnp.where(low, pltpu.roll(cpart, CHUNK, 1), hpart),
-            )
-        ):
-            hi, lo = two_terms(both[dirs:] + small)
-            msg[2 * t + i] = jnp.concatenate([both[:dirs], hi, lo], axis=0).astype(BF16)
-    for peer in walk_peers:
-        pltpu.make_async_remote_copy(
-            src_ref=msg.at[peer], dst_ref=got.at[w], send_sem=msend, recv_sem=mrecv,
-            device_id=(peer, b), device_id_type=MESH,
-        ).start()
+    gram = gram_of(0, panel[:, 0], nb) + gram_of(chunks, panel[:, 1], nb)
+    pltpu.make_async_copy(middle.at[others], middle.at[others], crecv).wait()
+    gram = gram + gram_of(1, middle[...], nb)
+    extra = jnp.concatenate([blank, small], axis=0)
+    for t in range(nw // 2):
+        cpart, hpart = halves_of(gram[:, t * LANES : (t + 1) * LANES])
+        base[2 * t] = jnp.where(low, cpart, pltpu.roll(hpart, CHUNK, 1)) + extra
+        base[2 * t + 1] = jnp.where(low, pltpu.roll(cpart, CHUNK, 1), hpart) + extra
+
+    outer = nb // 4
+    order = [(i, j) for i in range(outer) for j in range(2)]
+    order.sort(key=lambda s: min(s[0], outer - s[0]) + s[1])
+    for i, j in order:
+        to = lax.rem(b // 4 + i, outer) * 2 + lax.rem(lax.rem(b, 4) // 2 + j, 2)
+        for src in (2 * to, 2 * to + 1):
+
+            @pl.when(src != b)
+            def _():
+                pltpu.make_async_copy(tail.at[src], tail.at[src], brecv.at[src]).wait()
+
+        both = base[to] + jnp.concatenate(
+            halves_of(gram_of(2, tail[pl.ds(2 * to, 2)], 2)), axis=1
+        )
+        hi, lo = two_terms(both[dirs:])
+        msg[to] = jnp.concatenate([both[:dirs], hi, lo], axis=0).astype(BF16)
+
+        @pl.when(to != w)
+        def _():
+            pltpu.make_async_remote_copy(
+                src_ref=msg.at[to], dst_ref=got.at[w], send_sem=msend, recv_sem=mrecv,
+                device_id=(to, b), device_id_type=MESH,
+            ).start()
+
     got[w] = msg[w]
 
     pltpu.make_async_copy(panel.at[others], panel.at[others], asend).wait()
+    pltpu.make_async_copy(middle.at[others], middle.at[others], csend).wait()
     pltpu.make_async_copy(tail.at[others], tail.at[others], bsend).wait()
     groups = pl.ds(0, nw - 1)
     pltpu.make_async_copy(got.at[groups], got.at[groups], mrecv).wait()
@@ -280,23 +297,28 @@
                 pltpu.VMEM((rows, cols), BF16),
                 pltpu.VMEM((dirs, cols), BF16),
                 pltpu.VMEM((1, rows), F32),
-                pltpu.VMEM((nb, EARLY + 1, dirs, LANES), BF16),
+                pltpu.VMEM((nb, 2, dirs, LANES), BF16),
+                pltpu.VMEM((nb, dirs, LANES), BF16),
                 pltpu.VMEM((nb, dirs, LANES), BF16),
                 pltpu.VMEM((chunks + 1, 4 * dirs + 16, LANES), BF16),
+                pltpu.VMEM((nw, dirs + 8, LANES), F32),
                 pltpu.VMEM((nw, dirs + 16, LANES), BF16),
                 pltpu.VMEM((nw, dirs + 16, LANES), BF16),
                 pltpu.VMEM((nw, 8, LANES), F32),
                 dma((chunks * SPLIT,)),
                 dma((chunks * SPLIT,)),
-                dma((SPLIT,)),
+                dma((2 * SPLIT,)),
+                dma((nb,)),
             ]
-            + [dma(())] * 7,
+            + [dma(())] * 8,
             compiler_params=pltpu.CompilerParams(
                 collective_id=0, has_side_effects=True, vmem_limit_bytes=53 << 20
             ),
             name="pencil",
         )(
-            derivs, energy_grads, directions, local_energy.reshape(1, rows), widths, live_rows
+            derivs, energy_grads, directions,
+            pltpu.with_memory_space_constraint(local_energy.reshape(1, rows), pltpu.HBM),
+            widths, live_rows,
         )
         return out[:, CHUNK:], out[:, :CHUNK]
 

time: 29.2 us -> 25.5 us (0.87)
  Pallas kernels: 25.8 us -> 22.8 us
  local copies, waits for them, and re-layouts: 1.35 us -> 0.68 us
    pallas_call x1, Pallas kernels: 25.8 us -> 22.8 us  [per_device(): pl.pallas_call(functools.partial(pencil_kernel, nw, nb), out_shape=jax.Sh...]
    unnamed x2 -> x0, local copies, waits for them, and re-layouts: 0.67 us -> none
where the time goes in v3:
time: 25.5 us; the launch traced here: 25.4 us
  Pallas kernels  22.8 us (89%)
  between operations  1.93 us (8%)
  local copies, waits for them, and re-layouts  0.68 us (3%)
    pallas_call x1, Pallas kernels, per_device(): pl.pallas_call(functools.partial(pencil_kernel, nw, nb), out_shape=jax.Sh...  22.8 us
    slice x1, local copies, waits for them, and re-layouts, per_device(): return (out[:, CHUNK:], out[:, :CHUNK])  0.68 us

profile of v3, /device:TPU:1, one launch (start us, length us, event | category | flops | bytes accessed | tf_op | source)
XLA Modules:
  0.0 25.4 jit_solution(17152332744478973965)
XLA Ops:
  1.9 22.8 %pencil.1 = f32[32,128]{1,0:T(8,128)S(1)} custom-call(bf16[192,25600]{1,0:T(8,128)(2,1)} %d_hbm.1, bf16[192,25600]{1,0:T(8,128)(2,1)} %e_hbm.1, bf16[32,25600]{1,0:T(8,128)(2,1)} %v_hbm.1, f32[1,192]{1,0:T(1,128)} %bitcast.1, s32[1]{0:T(128)S(6)} %copy.8.wid_ref, s32[1]{0:T(128)S(6)} %copy.9.live_ref), custom_call_target="tpu_custom_call" | custom-call | tf_op jit(solution)/shard_map/pencil/pallas_call | solution.py:290
  24.7 0.7 %fusion = (f32[32,64]{1,0:T(8,128)}, f32[32,64]{1,0:T(8,128)}) fusion(f32[32,128]{1,0:T(8,128)S(1)} %pencil.1), kind=kLoop, calls=%fused_computation | loop fusion | bytes 32768 | tf_op jit(solution)/shard_map/slice | solution.py:323

commit v4 on v3

--- a/solution.py
+++ b/solution.py
@@ -42,8 +42,8 @@
 
 def pencil_kernel(
     nw, nb, d_hbm, e_hbm, v_hbm, en_hbm, wid_ref, live_ref, o_ref,
-    dv, ev, vv, en_ref, panel, middle, tail, lhs, base, msg, got, vecs,
-    dsem, esem, vsem, brecv, ensem, asend, arecv, csend, crecv, bsend, msend, mrecv,
+    dv, ev, vv, en_ref, panel, tail, lhs, msg, got, vecs,
+    dsem, esem, vsem, arecv, brecv, ensem, asend, csend, bsend, msend, mrecv,
 ):
     w = lax.axis_index("walk")
     b = lax.axis_index("blk")
@@ -163,7 +163,7 @@
     def send_all(buf, send_sem, recv_sem):
         for peer in blk_peers:
             pltpu.make_async_remote_copy(
-                src_ref=buf.at[b], dst_ref=buf.at[b], send_sem=send_sem, recv_sem=recv_sem,
+                src_ref=buf, dst_ref=buf, send_sem=send_sem, recv_sem=recv_sem.at[b // 4],
                 device_id=(w, peer), device_id_type=MESH,
             ).start()
 
@@ -178,18 +178,20 @@
     )
     en_copy.wait()
     d0, e0, g0 = panels(0, s0, common)
-    panel[b, 0] = g0
-    panel[b, 1] = shift.astype(BF16)
+    panel[b, dirs : 2 * dirs] = g0
+    panel[b, 2 * dirs :] = (
+        shift[: dirs // 2] + pltpu.roll(shift[dirs // 2 :], CHUNK, 1)
+    ).astype(BF16)
     pl.semaphore_wait(barrier, nw - 1 + nb - 1)
-    send_all(panel, asend, arecv)
+    send_all(panel.at[b, dirs:], asend, arecv)
 
     d1, e1, g1 = panels(1, project(1), common)
-    middle[b] = g1
-    send_all(middle, csend, crecv)
+    panel[b, :dirs] = g1
+    send_all(panel.at[b, :dirs], csend, arecv)
 
     d2, e2, g2 = panels(2, project(2), common)
     tail[b] = g2
-    send_all(tail, bsend, brecv.at[b])
+    send_all(tail.at[b], bsend, brecv)
 
     lhs[chunks] = jnp.concatenate(
         [blank, blank, mark(1, 0, 2), blank, blank, mark(1, 2, 4)], axis=0
@@ -202,9 +204,9 @@
         row8 == 5, esum, jnp.where(row8 == 6, live_rows.astype(F32), 0.0)
     )
 
-    def gram_of(c, block, count):
+    def gram_of(c, block):
         return lax.dot_general(
-            lhs[c], block.reshape(count * dirs, LANES), NT, preferred_element_type=F32
+            lhs[c], block.reshape(4 * dirs, LANES), NT, preferred_element_type=F32
         )
 
     def halves_of(tile):
@@ -213,45 +215,48 @@
             for part in (tile[:tall], tile[tall:])
         ]
 
+    def arrival(buf, sem, t):
+        def take(count):
+            part = buf.at[pl.ds(4 * t, count)]
+            pltpu.make_async_copy(part, part, sem.at[t]).wait()
+
+        pl.when(t == b // 4)(lambda: take(3))
+        pl.when(t != b // 4)(lambda: take(4))
+
+    for t in range(nb // 4):
+        quad = slice(4 * t, 4 * t + 4)
+        arrival(panel, arecv, t)
+        packed = panel[quad, 2 * dirs :].astype(F32)
+        packed = jnp.concatenate([packed, pltpu.roll(packed, CHUNK, 2)], axis=1).astype(BF16)
+        early = (
+            gram_of(0, panel[quad, dirs : 2 * dirs])
+            + gram_of(chunks, packed)
+            + gram_of(1, panel[quad, :dirs])
+        )
+        arrival(tail, brecv, t)
+        cpart, hpart = halves_of(early + gram_of(2, tail[quad]))
+        for i, both in enumerate(
+            (
+                jnp.where(low, cpart, pltpu.roll(hpart, CHUNK, 1)),
+                jnp.where(low, pltpu.roll(cpart, CHUNK, 1), hpart),
+            )
+        ):
+            to = 2 * t + i
+            hi, lo = two_terms(both[dirs:] + small)
+            msg[to] = jnp.concatenate([both[:dirs], hi, lo], axis=0).astype(BF16)
+
+            @pl.when(to != w)
+            def _():
+                pltpu.make_async_remote_copy(
+                    src_ref=msg.at[to], dst_ref=got.at[w], send_sem=msend, recv_sem=mrecv,
+                    device_id=(to, b), device_id_type=MESH,
+                ).start()
+
+    got[w] = msg[w]
+
     others = pl.ds(0, nb - 1)
-    pltpu.make_async_copy(panel.at[others], panel.at[others], arecv).wait()
-    gram = gram_of(0, panel[:, 0], nb) + gram_of(chunks, panel[:, 1], nb)
-    pltpu.make_async_copy(middle.at[others], middle.at[others], crecv).wait()
-    gram = gram + gram_of(1, middle[...], nb)
-    extra = jnp.concatenate([blank, small], axis=0)
-    for t in range(nw // 2):
-        cpart, hpart = halves_of(gram[:, t * LANES : (t + 1) * LANES])
-        base[2 * t] = jnp.where(low, cpart, pltpu.roll(hpart, CHUNK, 1)) + extra
-        base[2 * t + 1] = jnp.where(low, pltpu.roll(cpart, CHUNK, 1), hpart) + extra
-
-    outer = nb // 4
-    order = [(i, j) for i in range(outer) for j in range(2)]
-    order.sort(key=lambda s: min(s[0], outer - s[0]) + s[1])
-    for i, j in order:
-        to = lax.rem(b // 4 + i, outer) * 2 + lax.rem(lax.rem(b, 4) // 2 + j, 2)
-        for src in (2 * to, 2 * to + 1):
-
-            @pl.when(src != b)
-            def _():
-                pltpu.make_async_copy(tail.at[src], tail.at[src], brecv.at[src]).wait()
-
-        both = base[to] + jnp.concatenate(
-            halves_of(gram_of(2, tail[pl.ds(2 * to, 2)], 2)), axis=1
-        )
-        hi, lo = two_terms(both[dirs:])
-        msg[to] = jnp.concatenate([both[:dirs], hi, lo], axis=0).astype(BF16)
-
-        @pl.when(to != w)
-        def _():
-            pltpu.make_async_remote_copy(
-                src_ref=msg.at[to], dst_ref=got.at[w], send_sem=msend, recv_sem=mrecv,
-                device_id=(to, b), device_id_type=MESH,
-            ).start()
-
-    got[w] = msg[w]
-
-    pltpu.make_async_copy(panel.at[others], panel.at[others], asend).wait()
-    pltpu.make_async_copy(middle.at[others], middle.at[others], csend).wait()
+    for part, sem in ((panel.at[others, dirs:], asend), (panel.at[others, :dirs], csend)):
+        pltpu.make_async_copy(part, part, sem).wait()
     pltpu.make_async_copy(tail.at[others], tail.at[others], bsend).wait()
     groups = pl.ds(0, nw - 1)
     pltpu.make_async_copy(got.at[groups], got.at[groups], mrecv).wait()
@@ -297,20 +302,19 @@
                 pltpu.VMEM((rows, cols), BF16),
                 pltpu.VMEM((dirs, cols), BF16),
                 pltpu.VMEM((1, rows), F32),
-                pltpu.VMEM((nb, 2, dirs, LANES), BF16),
-                pltpu.VMEM((nb, dirs, LANES), BF16),
+                pltpu.VMEM((nb, 2 * dirs + dirs // 2, LANES), BF16),
                 pltpu.VMEM((nb, dirs, LANES), BF16),
                 pltpu.VMEM((chunks + 1, 4 * dirs + 16, LANES), BF16),
-                pltpu.VMEM((nw, dirs + 8, LANES), F32),
                 pltpu.VMEM((nw, dirs + 16, LANES), BF16),
                 pltpu.VMEM((nw, dirs + 16, LANES), BF16),
                 pltpu.VMEM((nw, 8, LANES), F32),
                 dma((chunks * SPLIT,)),
                 dma((chunks * SPLIT,)),
                 dma((2 * SPLIT,)),
-                dma((nb,)),
+                dma((nb // 4,)),
+                dma((nb // 4,)),
             ]
-            + [dma(())] * 8,
+            + [dma(())] * 6,
             compiler_params=pltpu.CompilerParams(
                 collective_id=0, has_side_effects=True, vmem_limit_bytes=53 << 20
             ),

time: 25.5 us -> 25 us (0.980)
  the two profiles are of different devices: /device:TPU:1 before, /device:TPU:7 now
where the time goes in v4:
time: 25 us; the launch traced here: 24.9 us
  Pallas kernels  22.3 us (89%)
  between operations  1.93 us (8%)
  local copies, waits for them, and re-layouts  0.68 us (3%)
    pallas_call x1, Pallas kernels, per_device(): pl.pallas_call(functools.partial(pencil_kernel, nw, nb), out_shape=jax.Sh...  22.3 us
    slice x1, local copies, waits for them, and re-layouts, per_device(): return (out[:, CHUNK:], out[:, :CHUNK])  0.68 us

profile of v4, /device:TPU:7, one launch (start us, length us, event | category | flops | bytes accessed | tf_op | source)
XLA Modules:
  0.0 24.9 jit_solution(10000888158072346951)
XLA Ops:
  1.9 22.3 %pencil.1 = f32[32,128]{1,0:T(8,128)S(1)} custom-call(bf16[192,25600]{1,0:T(8,128)(2,1)} %d_hbm.1, bf16[192,25600]{1,0:T(8,128)(2,1)} %e_hbm.1, bf16[32,25600]{1,0:T(8,128)(2,1)} %v_hbm.1, f32[1,192]{1,0:T(1,128)} %bitcast.1, s32[1]{0:T(128)S(6)} %copy.8.wid_ref, s32[1]{0:T(128)S(6)} %copy.9.live_ref), custom_call_target="tpu_custom_call" | custom-call | tf_op jit(solution)/shard_map/pencil/pallas_call | solution.py:295
  24.2 0.7 %fusion = (f32[32,64]{1,0:T(8,128)}, f32[32,64]{1,0:T(8,128)}) fusion(f32[32,128]{1,0:T(8,128)S(1)} %pencil.1), kind=kLoop, calls=%fused_computation | loop fusion | bytes 32768 | tf_op jit(solution)/shard_map/slice | solution.py:327

commit v5 on v4

--- a/solution.py
+++ b/solution.py
@@ -142,11 +142,10 @@
             e = pltpu.roll(e, CHUNK, 1)
         return jnp.where(low & (c * CHUNK + lane < live_rows), e, 0.0)
 
-    def panels(c, s, common):
+    def panels(c, s, common, erow):
         walker = c * CHUNK + jnp.where(low, lane, lane - CHUNK)
         d = jnp.where(walker < live_rows, s - common, 0.0)
-        erow = energies(c)
-        return d, erow, (d + pltpu.roll(d * erow, CHUNK, 1)).astype(BF16)
+        return d, (d + pltpu.roll(d * erow, CHUNK, 1)).astype(BF16)
 
     def own_side(c, d, erow):
         own = jnp.where(low, d, 0.0)
@@ -177,7 +176,8 @@
         lane == 0, phi, jnp.where(lane == 1, plo, jnp.where(lane == 2, qhi, jnp.where(lane == 3, qlo, 0.0)))
     )
     en_copy.wait()
-    d0, e0, g0 = panels(0, s0, common)
+    e0, e1, e2 = energies(0), energies(1), energies(2)
+    d0, g0 = panels(0, s0, common, e0)
     panel[b, dirs : 2 * dirs] = g0
     panel[b, 2 * dirs :] = (
         shift[: dirs // 2] + pltpu.roll(shift[dirs // 2 :], CHUNK, 1)
@@ -185,19 +185,20 @@
     pl.semaphore_wait(barrier, nw - 1 + nb - 1)
     send_all(panel.at[b, dirs:], asend, arecv)
 
-    d1, e1, g1 = panels(1, project(1), common)
+    d1, g1 = panels(1, project(1), common, e1)
     panel[b, :dirs] = g1
     send_all(panel.at[b, :dirs], csend, arecv)
-
-    d2, e2, g2 = panels(2, project(2), common)
-    tail[b] = g2
-    send_all(tail.at[b], bsend, brecv)
 
     lhs[chunks] = jnp.concatenate(
         [blank, blank, mark(1, 0, 2), blank, blank, mark(1, 2, 4)], axis=0
     ).astype(BF16)
-    rv = own_side(0, d0, e0) + own_side(1, d1, e1) + own_side(2, d2, e2)
-    rv = rv + exact_dot(mark(4, 0, 2), shift, NT)
+    rv = own_side(0, d0, e0) + own_side(1, d1, e1) + exact_dot(mark(4, 0, 2), shift, NT)
+
+    d2, g2 = panels(2, project(2), common, e2)
+    tail[b] = g2
+    send_all(tail.at[b], bsend, brecv)
+
+    rv = rv + own_side(2, d2, e2)
     rv = jnp.concatenate([rv, jnp.zeros((8, LANES - dirs), F32)], axis=1)
     esum = jnp.sum(e0 + e1 + e2, axis=1, keepdims=True)
     small = rv + jnp.where(

time: 25 us -> 25.1 us (level)
  no operation moved by 1% of the time
where the time goes in v5:
time: 25.1 us; the launch traced here: 25 us
  Pallas kernels  22.4 us (89%)
  between operations  1.93 us (8%)
  local copies, waits for them, and re-layouts  0.68 us (3%)
    pallas_call x1, Pallas kernels, per_device(): pl.pallas_call(functools.partial(pencil_kernel, nw, nb), out_shape=jax.Sh...  22.4 us
    slice x1, local copies, waits for them, and re-layouts, per_device(): return (out[:, CHUNK:], out[:, :CHUNK])  0.68 us

profile of v5, /device:TPU:7, one launch (start us, length us, event | category | flops | bytes accessed | tf_op | source)
XLA Modules:
  0.0 25.0 jit_solution(14570463584807272175)
XLA Ops:
  1.9 22.4 %pencil.1 = f32[32,128]{1,0:T(8,128)S(1)} custom-call(bf16[192,25600]{1,0:T(8,128)(2,1)} %d_hbm.1, bf16[192,25600]{1,0:T(8,128)(2,1)} %e_hbm.1, bf16[32,25600]{1,0:T(8,128)(2,1)} %v_hbm.1, f32[1,192]{1,0:T(1,128)} %bitcast.1, s32[1]{0:T(128)S(6)} %copy.8.wid_ref, s32[1]{0:T(128)S(6)} %copy.9.live_ref), custom_call_target="tpu_custom_call" | custom-call | tf_op jit(solution)/shard_map/pencil/pallas_call | solution.py:296
  24.3 0.7 %fusion = (f32[32,64]{1,0:T(8,128)}, f32[32,64]{1,0:T(8,128)}) fusion(f32[32,128]{1,0:T(8,128)S(1)} %pencil.1), kind=kLoop, calls=%fused_computation | loop fusion | bytes 32768 | tf_op jit(solution)/shard_map/slice | solution.py:328
